TPU v7x, 256 devices: a whole 4x4x8 slice. The times are simulated.
256 devices in a mesh: seq: 32 (over y, x, core), tensor: 8 (over z).
Axes of the slice: x: 4, y: 4, z: 8, core: 2. Of those that a mesh axis runs over, the one named last changes fastest.
Arguments:
- queries: bfloat16 [4096, 8192], P('seq', 'tensor'), may hold values from -6 to 6
- key_vectors: bfloat16 [4096, 8192], P('seq', 'tensor'), may hold values from -6 to 6
- value_rows: bfloat16 [4096, 8192], P('seq', 'tensor'), may hold values from -6 to 6
- gate_logits: bfloat16 [4096, 8192], P('seq', 'tensor'), may hold values from -6 to 6
- log_decay: float32 [4096, 64], P('seq', 'tensor'), may hold values from -0.73 to 0, as said below
- initial_state: float32 [64, 128, 128], P('tensor'), may hold values from -192 to 192
- norm_gain: float32 [8192], P('tensor'), may hold values from 0.25 to 1.75
- out_weight: bfloat16 [8192, 6144], P('tensor', 'seq'), may hold values from -0.0625 to 0.0625
Outputs:
- mixed: float32 [4096, 6144], P('seq', 'tensor')
Inputs may be any that keep to these rules, and one draw needn't show every extreme that they name: `log_decay`: every entry is negative.
All inputs are finite; a program needn't handle non-finite values.
Results may differ from a plain program's by a relative error of at most 0.0075.
Values may be sent and summed in bfloat16 or wider, within the bound.
No kernel may reach another device: no remote copies, remote signals or barrier semaphores. Data moves between devices by JAX's collectives and lax.ppermute only.
A program may use at most 128 MiB of HBM per device.

v0:
```python
import jax
import jax.numpy as jnp
from jax import lax
from jax.sharding import PartitionSpec as P

HIGH = lax.Precision.HIGHEST


def entering(array, axis, combine, identity):
    length, mine = (lax.axis_size(axis), lax.axis_index(axis))
    everything = jax.tree.map(lambda part: lax.all_gather(part, axis), array)
    start = jax.tree.map(
        lambda part, zero: jnp.broadcast_to(jnp.asarray(zero, part.dtype), part.shape),
        array,
        identity,
    )

    def hop(k, before):
        reached = k < mine
        new = combine(before, jax.tree.map(lambda part: part[k], everything))
        return jax.tree.map(lambda a, b: jnp.where(reached, a, b), new, before)

    return lax.fori_loop(0, length, hop, start)


def block_step(state, pieces):
    queries_b, keys_b, values_b, decay_b = pieces
    cumulative_memory = jnp.cumsum(decay_b, axis=0)
    total = cumulative_memory[-1]
    carried = jnp.exp(cumulative_memory)[:, :, None] * jnp.einsum(
        "thd,hde->the", queries_b.astype(jnp.float32), state, precision=HIGH
    )
    scores = jnp.einsum("thd,shd->hts", queries_b, keys_b, preferred_element_type=jnp.float32)
    length = cumulative_memory.shape[0]
    lower = jnp.tril(jnp.ones((length, length), dtype=bool))[None]
    spread = cumulative_memory.T[:, :, None] - cumulative_memory.T[:, None, :]
    weights = jnp.where(lower, jnp.exp(jnp.where(lower, spread, 0.0)), 0.0)
    mixes = (scores * weights).astype(jnp.bfloat16)
    local = jnp.einsum("hts,she->the", mixes, values_b, preferred_element_type=jnp.float32)
    scaled = keys_b.astype(jnp.float32) * jnp.exp(total[None, :] - cumulative_memory)[:, :, None]
    new_state = jnp.exp(total)[:, None, None] * state + jnp.einsum(
        "shd,she->hde", scaled, values_b.astype(jnp.float32), precision=HIGH
    )
    return (new_state, carried + local)


def normalize(attended, norm_gain, gate_logits):
    mean_square = jnp.mean(attended * attended, axis=-1, keepdims=True)
    normalized_output = attended * lax.rsqrt(mean_square + 1e-05)
    flat = normalized_output.reshape(attended.shape[0], -1)
    gated = flat * norm_gain[None, :] * jax.nn.sigmoid(gate_logits.astype(jnp.float32))
    return gated.astype(jnp.bfloat16)


def chain_link(earlier, later):
    return (earlier[0] * later[0], later[0][:, None, None] * earlier[1] + later[1])


def pack(rates, state):
    heads = state.shape[0]
    flat = state.reshape(heads, -1)
    lanes = jnp.broadcast_to(rates[:, None], (heads, 128))
    return jnp.concatenate([flat, lanes], axis=1)


def link_packed(earlier, later):
    width = later.shape[1] - 128
    later_rate = later[:, width : width + 1]
    state = later_rate * earlier[:, :width] + later[:, :width]
    rate = earlier[:, width:] * later[:, width:]
    return jnp.concatenate([state, rate], axis=1)


def carried_in(rates, state, initial_state):
    length, mine = (lax.axis_size("seq"), lax.axis_index("seq"))
    own = pack(rates, state)
    shifted = lax.ppermute(own, "seq", [(i, i + 1) for i in range(length - 1)])
    first = pack(jnp.ones_like(rates), initial_state)
    current = jnp.where(mine == 0, first, shifted)
    step = 1
    while step < length:
        earlier = lax.ppermute(current, "seq", [(i, i + step) for i in range(length - step)])
        current = jnp.where(mine >= step, link_packed(earlier, current), current)
        step *= 2
    width = current.shape[1] - 128
    return current[:, :width].reshape(state.shape)


def per_device(
    queries, key_vectors, value_rows, gate_logits, log_decay, initial_state, norm_gain, out_weight
):
    rows_here = queries.shape[0]
    head_count = log_decay.shape[1]
    head_dim = initial_state.shape[1]
    block_len = min(512, rows_here)
    block_count = rows_here // block_len

    def shaped(array):
        return array.reshape(block_count, block_len, head_count, head_dim)

    zero_state = jnp.zeros((head_count, head_dim, head_dim), jnp.float32)
    decay_blocks = log_decay.reshape(block_count, block_len, head_count)
    device_state, outputs = lax.scan(
        block_step,
        zero_state,
        (shaped(queries), shaped(key_vectors), shaped(value_rows), decay_blocks),
    )
    local_out = outputs.reshape(rows_here, head_count, head_dim)
    through = jnp.cumsum(log_decay, axis=0)
    shard_fading_rates = jnp.exp(through[-1])
    incoming = carried_in(shard_fading_rates, device_state, initial_state)
    query_float = queries.reshape(rows_here, head_count, head_dim).astype(jnp.float32)
    inherited = jnp.exp(through)[:, :, None] * jnp.einsum(
        "thd,hde->the", query_float, incoming, precision=HIGH
    )
    attended = local_out + inherited
    hidden = normalize(attended, norm_gain, gate_logits)
    seq_len, tensor_len = (lax.axis_size("seq"), lax.axis_size("tensor"))
    col_blocks = seq_len // tensor_len
    route = []
    for s in range(seq_len):
        for t in range(tensor_len):
            source = (col_blocks * t + s // tensor_len) * tensor_len + s % tensor_len
            route.append((source, s * tensor_len + t))
    placed = lax.ppermute(out_weight, ("seq", "tensor"), route)
    columns = lax.all_gather(placed, "seq", axis=0, tiled=True)
    columns = columns.reshape(col_blocks, -1, columns.shape[1])
    full_hidden = lax.all_gather(hidden, "tensor", axis=1, tiled=True)
    mixed = jnp.einsum("tk,rkc->trc", full_hidden, columns, preferred_element_type=jnp.float32)
    mixed = mixed.reshape(rows_here, -1)
    return mixed


def solution(mesh):
    return jax.shard_map(
        per_device,
        mesh=mesh,
        in_specs=(
            P("seq", "tensor"),
            P("seq", "tensor"),
            P("seq", "tensor"),
            P("seq", "tensor"),
            P("seq", "tensor"),
            P("tensor", None, None),
            P("tensor"),
            P("tensor", "seq"),
        ),
        out_specs=P("seq", "tensor"),
        check_vma=False,
    )
```

profile of v0, /device:TPU:8, one launch (start us, length us, event | category | flops | bytes accessed | tf_op | source)
XLA Modules:
  0.0 229.9 jit_solution(4857555923900355773)
XLA Ops:
  6.5 0.8 copy.36
  7.4 0.2 reduce_window_sum.13
  7.7 1.1 copy.54
  8.8 1.4 fusion.4
  10.2 0.3 copy.91
  10.5 0.1 broadcast_in_dim.56
  10.6 1.9 collective-permute-start
  12.5 1.4 copy.92
  13.9 9.3 %collective-permute-done = f32[8,16512]{1,0:T(8,128)S(1)} collective-permute-done((f32[8,16512]{1,0:T(8,128)S(1)}, f32[8,16512]{1,0:T(8,128)S(1)}, u32[]{:S(2)}, u32[]{:S(2)}) %collective-permute-start) | collective-permute-done | bytes 528416 | tf_op jit(solution)/shard_map/ppermute | solution.py:77
  23.2 0.1 pad_select_fusion
  23.3 1.9 collective-permute-start.1
  25.2 0.1 slice_reduce_fusion.4
  25.4 10.6 %collective-permute-done.1 = f32[8,16512]{1,0:T(8,128)S(1)} collective-permute-done((f32[8,16512]{1,0:T(8,128)S(1)}, f32[8,16512]{1,0:T(8,128)S(1)}, u32[]{:S(2)}, u32[]{:S(2)}) %collective-permute-start.1) | collective-permute-done | bytes 528416 | tf_op jit(solution)/shard_map/ppermute | solution.py:82
  36.0 0.1 slice_add_fusion.3
  36.1 0.1 maximum_select_fusion
  36.2 1.9 collective-permute-start.2
  38.1 2.4 %collective-permute-start.6 = (bf16[1024,192]{0,1:T(8,128)(2,1)}, bf16[1024,192]{0,1:T(8,128)(2,1)S(1)}, u32[]{:S(2)}, u32[]{:S(2)}) collective-permute-start(bf16[1024,192]{0,1:T(8,128)(2,1)} %param.15), channel_id=1, source_target_pairs={{0,0},{32,1},{64,2},{96,3},{128,4},{160,5},{192,6},{224,7},{1,8},{... | collective-permute-start | bytes 1179656 | tf_op jit(solution)/shard_map/ppermute | solution.py:125
  40.5 39.4 %collective-permute-done.6 = bf16[1024,192]{0,1:T(8,128)(2,1)S(1)} collective-permute-done((bf16[1024,192]{0,1:T(8,128)(2,1)}, bf16[1024,192]{0,1:T(8,128)(2,1)S(1)}, u32[]{:S(2)}, u32[]{:S(2)}) %collective-permute-start.6) | collective-permute-done | bytes 393248 | tf_op jit(solution)/shard_map/ppermute | solution.py:125
  79.8 0.7 copy-done.2
  80.6 0.1 slice_reduce_fusion.3
  80.8 0.1 slice_add_fusion.2
  80.9 0.1 maximum_select_fusion.1
  81.0 1.9 collective-permute-start.3
  82.9 0.1 slice_reduce_fusion.2
  83.0 15.8 %collective-permute-done.3 = f32[8,16512]{1,0:T(8,128)S(1)} collective-permute-done((f32[8,16512]{1,0:T(8,128)S(1)}, f32[8,16512]{1,0:T(8,128)S(1)}, u32[]{:S(2)}, u32[]{:S(2)}) %collective-permute-start.3) | collective-permute-done | bytes 528416 | tf_op jit(solution)/shard_map/ppermute | solution.py:82
  98.8 0.1 slice_add_fusion.1
  99.0 0.1 maximum_select_fusion.2
  99.1 1.9 collective-permute-start.4
  101.0 0.1 slice_reduce_fusion.1
  101.1 20.9 %collective-permute-done.4 = f32[8,16512]{1,0:T(8,128)S(1)} collective-permute-done((f32[8,16512]{1,0:T(8,128)S(1)}, f32[8,16512]{1,0:T(8,128)S(1)}, u32[]{:S(2)}, u32[]{:S(2)}) %collective-permute-start.4) | collective-permute-done | bytes 528416 | tf_op jit(solution)/shard_map/ppermute | solution.py:82
  122.0 0.1 slice_add_fusion
  122.1 0.1 maximum_select_fusion.3
  122.2 1.3 collective-permute-start.5
  123.6 0.1 copy.37
  123.7 0.7 fusion.2
  124.4 0.1 slice_reduce_fusion
  124.5 10.8 %collective-permute-done.5 = f32[8,16512]{1,0:T(8,128)S(1)} collective-permute-done((f32[8,16512]{1,0:T(8,128)S(1)}, f32[8,16512]{1,0:T(8,128)S(1)}, u32[]{:S(2)}, u32[]{:S(2)}) %collective-permute-start.5) | collective-permute-done | bytes 528416 | tf_op jit(solution)/shard_map/ppermute | solution.py:82
  135.3 0.1 fusion.10
  135.4 0.1 fusion.9
  135.5 0.6 fusion.3
  136.1 0.5 multiply_reduce_fusion
  136.7 0.2 copy.50
  136.9 0.9 multiply_convert_fusion
  137.8 32.2 %all-gather.5.cloned.1.call-done = bf16[32768,192]{0,1:T(8,128)(2,1)} async-done(((bf16[1024,192]{0,1:T(8,128)(2,1)}), bf16[32768,192]{0,1:T(8,128)(2,1)}) %all-gather.5.cloned.1.call-update) | async-done | bytes 12582928 | tf_op jit(solution)/shard_map/all_gather | solution.py:126
  170.1 21.3 %reshape.82 = bf16[4,8192,192]{1,0,2:T(4,128)(2,1)} reshape(bf16[32768,192]{0,1:T(8,128)(2,1)} %all-gather.5.cloned.1.call-done) | data formatting | bytes 25165824 | tf_op jit(solution)/shard_map/reshape | solution.py:127
  191.4 14.5 %copy.51 = bf16[4,192,8192]{2,1,0:T(8,128)(2,1)} copy(bf16[4,192,8192]{2,0,1:T(4,128)(2,1)} %bitcast.80) | data formatting | bytes 25165824 | tf_op jit(solution)/shard_map/tk,rkc->trc/dot_general | solution.py:129
  205.9 6.9 %all-gather.3.cloned.1.call-done = bf16[128,8192]{1,0:T(8,128)(2,1)} async-done(((bf16[128,1024]{1,0:T(8,128)(2,1)}), bf16[128,8192]{1,0:T(8,128)(2,1)}) %all-gather.3.cloned.1.call-update) | async-done | bytes 2097168 | tf_op jit(solution)/shard_map/all_gather | solution.py:128
  212.8 10.2 %fusion.41 = f32[128,768]{1,0:T(8,128)} fusion(bf16[128,8192]{1,0:T(8,128)(2,1)} %all-gather.3.cloned.1.call-done, bf16[768,8192]{1,0:T(8,128)(2,1)} %bitcast.79), kind=kOutput, calls=%fused_computation.78 | convolution fusion | flops 1610612736 | bytes 15073280 | tf_op jit(solution)/shard_map/tk,rkc->trc/dot_general | solution.py:129
  (28 shorter events, 0.4 us)
Async XLA Ops:
  6.5 117.2 %copy-start = (bf16[128,1024]{1,0:T(8,128)(2,1)S(1)}, bf16[128,1024]{1,0:T(8,128)(2,1)}, u32[]{:S(2)}) copy-start(bf16[128,1024]{1,0:T(8,128)(2,1)} %param.8) | copy-start | bytes 786436
  6.5 163.5 %all-gather.5.cloned.1.call-start = ((), (), s32[]{:S(2)}) async-start(), calls=%async_computation.1 | async-start | bytes 12976128 | tf_op jit(solution)/shard_map/all_gather | solution.py:126
  7.5 128.6 %copy-start.1 = (bf16[128,1024]{1,0:T(8,128)(2,1)S(1)}, bf16[128,1024]{1,0:T(8,128)(2,1)}, u32[]{:S(2)}) copy-start(bf16[128,1024]{1,0:T(8,128)(2,1)} %param.10) | copy-start | bytes 786436
  10.6 12.7 %collective-permute-start = (f32[8,16512]{1,0:T(8,128)S(1)}, f32[8,16512]{1,0:T(8,128)S(1)}, u32[]{:S(2)}, u32[]{:S(2)}) collective-permute-start(f32[8,16512]{1,0:T(8,128)S(1)} %pad_maximum_fusion), channel_id=1, source_target_pairs={{0,8},{8,16},{16,24},{24,32},{32,40},{40,48},{48,56},{56,64},{64,7... | collective-permute-start | bytes 1585160 | tf_op jit(solution)/shard_map/ppermute | solution.py:77
  12.5 124.4 %copy-start.3 = (bf16[128,1024]{1,0:T(8,128)(2,1)S(1)}, bf16[128,1024]{1,0:T(8,128)(2,1)}, u32[]{:S(2)}) copy-start(bf16[128,1024]{1,0:T(8,128)(2,1)} %param.11) | copy-start | bytes 786436
  12.5 124.4 %copy-start.4 = (f32[1024]{0:T(1024)S(1)}, f32[1024]{0:T(1024)}, u32[]{:S(2)}) copy-start(f32[1024]{0:T(1024)} %param.14) | copy-start | bytes 12292
  23.3 12.7 %collective-permute-start.1 = (f32[8,16512]{1,0:T(8,128)S(1)}, f32[8,16512]{1,0:T(8,128)S(1)}, u32[]{:S(2)}, u32[]{:S(2)}) collective-permute-start(f32[8,16512]{1,0:T(8,128)S(1)} %pad_select_fusion), channel_id=1, source_target_pairs={{0,8},{8,16},{16,24},{24,32},{32,40},{40,48},{48,56},{56,64},{64,7... | collective-permute-start | bytes 1585160 | tf_op jit(solution)/shard_map/ppermute | solution.py:82
  36.2 44.6 %collective-permute-start.2 = (f32[8,16512]{1,0:T(8,128)S(1)}, f32[8,16512]{1,0:T(8,128)S(1)}, u32[]{:S(2)}, u32[]{:S(2)}) collective-permute-start(f32[8,16512]{1,0:T(8,128)S(1)} %maximum_select_fusion), channel_id=1, source_target_pairs={{0,16},{8,24},{16,32},{24,40},{32,48},{40,56},{48,64},{56,72},{64,... | collective-permute-start | bytes 1585160 | tf_op jit(solution)/shard_map/ppermute | solution.py:82
  38.1 41.7 %collective-permute-start.6 = (bf16[1024,192]{0,1:T(8,128)(2,1)}, bf16[1024,192]{0,1:T(8,128)(2,1)S(1)}, u32[]{:S(2)}, u32[]{:S(2)}) collective-permute-start(bf16[1024,192]{0,1:T(8,128)(2,1)} %param.15), channel_id=1, source_target_pairs={{0,0},{32,1},{64,2},{96,3},{128,4},{160,5},{192,6},{224,7},{1,8},{... | collective-permute-start | bytes 1179656 | tf_op jit(solution)/shard_map/ppermute | solution.py:125
  79.8 0.7 copy-start.2
  80.6 132.2 %all-gather.3.cloned.1.call-start = ((), (), s32[]{:S(2)}) async-start(), calls=%async_computation | async-start | bytes 2359296 | tf_op jit(solution)/shard_map/all_gather | solution.py:128
  81.0 17.9 %collective-permute-start.3 = (f32[8,16512]{1,0:T(8,128)S(1)}, f32[8,16512]{1,0:T(8,128)S(1)}, u32[]{:S(2)}, u32[]{:S(2)}) collective-permute-start(f32[8,16512]{1,0:T(8,128)S(1)} %maximum_select_fusion.1), channel_id=1, source_target_pairs={{0,32},{8,40},{16,48},{24,56},{32,64},{40,72},{48,80},{56,88},{64,... | collective-permute-start | bytes 1585160 | tf_op jit(solution)/shard_map/ppermute | solution.py:82
  99.1 22.9 %collective-permute-start.4 = (f32[8,16512]{1,0:T(8,128)S(1)}, f32[8,16512]{1,0:T(8,128)S(1)}, u32[]{:S(2)}, u32[]{:S(2)}) collective-permute-start(f32[8,16512]{1,0:T(8,128)S(1)} %maximum_select_fusion.2), channel_id=1, source_target_pairs={{0,64},{8,72},{16,80},{24,88},{32,96},{40,104},{48,112},{56,120},{... | collective-permute-start | bytes 1585160 | tf_op jit(solution)/shard_map/ppermute | solution.py:82
  122.2 13.1 %collective-permute-start.5 = (f32[8,16512]{1,0:T(8,128)S(1)}, f32[8,16512]{1,0:T(8,128)S(1)}, u32[]{:S(2)}, u32[]{:S(2)}) collective-permute-start(f32[8,16512]{1,0:T(8,128)S(1)} %maximum_select_fusion.3), channel_id=1, source_target_pairs={{0,128},{8,136},{16,144},{24,152},{32,160},{40,168},{48,176},{56,1... | collective-permute-start | bytes 1585160 | tf_op jit(solution)/shard_map/ppermute | solution.py:82
Sparse Core Ops, SparseCore 0:
  80.7 89.2 all-gather.4
  171.8 40.9 all-gather.2
where the time goes:
time: 231 us; the launch traced here: 230 us
  waiting for transfers between devices  146 us (63%)
  local copies, waits for them, and re-layouts  41.3 us (18%)
  between operations  13.7 us (6%)
  matrix products  13.4 us (6%)
  starting transfers between devices  13.3 us (6%)
    ppermute x5, waiting for transfers between devices, carried_in(): lax.ppermute(current, 'seq', [(i, i + step) for i in range(length - step)])  58.1 us
    ppermute x1, waiting for transfers between devices, per_device(): placed = lax.ppermute(out_weight, ('seq', 'tensor'), route)  39.4 us
    all_gather x1, waiting for transfers between devices, per_device(): columns = lax.all_gather(placed, 'seq', axis=0, tiled=True)  32.2 us
    reshape x1, local copies, waits for them, and re-layouts, per_device(): columns = columns.reshape(col_blocks, -1, columns.shape[1])  21.3 us
    dot_general x1, local copies, waits for them, and re-layouts, per_device(): jnp.einsum('tk,rkc->trc', full_hidden, columns, preferred_element_type=jn...  14.5 us
    dot_general x1, matrix products, per_device(): jnp.einsum('tk,rkc->trc', full_hidden, columns, preferred_element_type=jn...  10.2 us
    ppermute x1, waiting for transfers between devices, carried_in(): shifted = lax.ppermute(own, 'seq', [(i, i + 1) for i in range(length - 1)])  9.3 us
    ppermute x5, starting transfers between devices, carried_in(): lax.ppermute(current, 'seq', [(i, i + step) for i in range(length - step)])  9 us
  transfers between devices with their start and end apart: 9, of which 8 were waited for; matrix products, arithmetic and copies ran while one was open for 18% of the time, Pallas kernels for 0%

commit v1 on v0

--- a/solution.py
+++ b/solution.py
@@ -4,6 +4,18 @@
 from jax.sharding import PartitionSpec as P
 
 HIGH = lax.Precision.HIGHEST
+
+
+def search_field_all(patch, dimension_no, frame_in):
+    formed, n_now = (lax.axis_size("tensor"), lax.axis_index("tensor"))
+    stack_in = list(map(lambda i0: (i0, (i0 - 1) % formed), range(formed)))
+    fresh = patch.shape[dimension_no]
+    right_arr = patch
+    value_now = frame_in(right_arr, n_now * fresh)
+    for it in range(1, formed):
+        right_arr = lax.ppermute(right_arr, axis_name="tensor", perm=stack_in)
+        value_now = value_now + frame_in(right_arr, (n_now + it) % formed * fresh)
+    return value_now
 
 
 def entering(array, axis, combine, identity):
@@ -125,8 +137,16 @@
     placed = lax.ppermute(out_weight, ("seq", "tensor"), route)
     columns = lax.all_gather(placed, "seq", axis=0, tiled=True)
     columns = columns.reshape(col_blocks, -1, columns.shape[1])
-    full_hidden = lax.all_gather(hidden, "tensor", axis=1, tiled=True)
-    mixed = jnp.einsum("tk,rkc->trc", full_hidden, columns, preferred_element_type=jnp.float32)
+    mixed = search_field_all(
+        hidden,
+        1,
+        lambda own_block, at: jnp.einsum(
+            "tk,rkc->trc",
+            own_block,
+            lax.dynamic_slice_in_dim(columns, at, own_block.shape[1], axis=1),
+            preferred_element_type=jnp.float32,
+        ),
+    )
     mixed = mixed.reshape(rows_here, -1)
     return mixed
 

time: 231 us -> 252 us (1.091)
  starting transfers between devices: 13.3 us -> 47.9 us
  waiting for transfers between devices: 146 us -> 139 us
  matrix products: 13.4 us -> 7.81 us
  local copies, waits for them, and re-layouts: 41.3 us -> 38.7 us
    ppermute x0 -> x7, starting transfers between devices: none -> 34.6 us  [search_field_all(): right_arr = lax.ppermute(right_arr, axis_name='tensor', perm=stack_in)]
    all_gather x1, waiting for transfers between devices: 32.2 us -> 0.01 us  [per_device(): columns = lax.all_gather(placed, 'seq', axis=0, tiled=True)]
    ppermute x0 -> x7, waiting for transfers between devices: none -> 31.7 us  [search_field_all(): right_arr = lax.ppermute(right_arr, axis_name='tensor', perm=stack_in)]
    dot_general x1 -> x0, local copies, waits for them, and re-layouts: 14.5 us -> none  [per_device(): jnp.einsum('tk,rkc->trc', full_hidden, columns, preferred_element_type=jn...]
    dot_general x1 -> x0, matrix products: 10.2 us -> none  [per_device(): jnp.einsum('tk,rkc->trc', full_hidden, columns, preferred_element_type=jn...]
    dynamic_slice x0 -> x1, local copies, waits for them, and re-layouts: none -> 7.49 us  [per_device(): lax.dynamic_slice_in_dim(columns, at, own_block.shape[1], axis=1)]
    all_gather x1 -> x0, waiting for transfers between devices: 6.95 us -> none  [per_device(): full_hidden = lax.all_gather(hidden, 'tensor', axis=1, tiled=True)]
    unnamed x0 -> x8, matrix products: none -> 4.61 us
  transfers between devices with their start and end apart: 9 -> 15, of which waited for: 8 -> 12; matrix products, arithmetic and copies ran while one was open for 18% -> 16% of each run, Pallas kernels for 0% -> 0%
where the time goes in v1:
time: 252 us; the launch traced here: 249 us
  waiting for transfers between devices  139 us (55%)
  starting transfers between devices  47.9 us (19%)
  local copies, waits for them, and re-layouts  38.7 us (15%)
  between operations  13.8 us (5%)
  matrix products  7.81 us (3%)
    ppermute x5, waiting for transfers between devices, carried_in(): lax.ppermute(current, 'seq', [(i, i + step) for i in range(length - step)])  58.1 us
    ppermute x1, waiting for transfers between devices, per_device(): placed = lax.ppermute(out_weight, ('seq', 'tensor'), route)  39 us
    ppermute x7, starting transfers between devices, search_field_all(): right_arr = lax.ppermute(right_arr, axis_name='tensor', perm=stack_in)  34.6 us
    ppermute x7, waiting for transfers between devices, search_field_all(): right_arr = lax.ppermute(right_arr, axis_name='tensor', perm=stack_in)  31.7 us
    reshape x1, local copies, waits for them, and re-layouts, per_device(): columns = columns.reshape(col_blocks, -1, columns.shape[1])  21.3 us
    ppermute x1, waiting for transfers between devices, carried_in(): shifted = lax.ppermute(own, 'seq', [(i, i + 1) for i in range(length - 1)])  10.4 us
    ppermute x5, starting transfers between devices, carried_in(): lax.ppermute(current, 'seq', [(i, i + step) for i in range(length - step)])  9.01 us
    dynamic_slice x1, local copies, waits for them, and re-layouts, per_device(): lax.dynamic_slice_in_dim(columns, at, own_block.shape[1], axis=1)  7.49 us
  transfers between devices with their start and end apart: 15, of which 12 were waited for; matrix products, arithmetic and copies ran while one was open for 16% of the time, Pallas kernels for 0%

profile of v1, /device:TPU:8, one launch (start us, length us, event | category | flops | bytes accessed | tf_op | source)
XLA Modules:
  0.0 249.2 jit_solution(13869286828896277173)
XLA Ops:
  6.5 0.8 copy.46
  7.6 1.1 copy.80
  8.8 1.4 fusion.4
  10.6 1.9 collective-permute-start
  12.9 10.4 %collective-permute-done = f32[8,16512]{1,0:T(8,128)S(1)} collective-permute-done((f32[8,16512]{1,0:T(8,128)S(1)}, f32[8,16512]{1,0:T(8,128)S(1)}, u32[]{:S(2)}, u32[]{:S(2)}) %collective-permute-start) | collective-permute-done | bytes 528416 | tf_op jit(solution)/shard_map/ppermute | solution.py:89
  23.4 1.9 collective-permute-start.1
  25.4 10.6 %collective-permute-done.1 = f32[8,16512]{1,0:T(8,128)S(1)} collective-permute-done((f32[8,16512]{1,0:T(8,128)S(1)}, f32[8,16512]{1,0:T(8,128)S(1)}, u32[]{:S(2)}, u32[]{:S(2)}) %collective-permute-start.1) | collective-permute-done | bytes 528416 | tf_op jit(solution)/shard_map/ppermute | solution.py:94
  36.2 1.9 collective-permute-start.2
  38.2 2.4 collective-permute-start.6
  40.5 39.0 %collective-permute-done.6 = bf16[1024,192]{0,1:T(8,128)(2,1)S(1)} collective-permute-done((bf16[1024,192]{0,1:T(8,128)(2,1)S(1)}, bf16[1024,192]{0,1:T(8,128)(2,1)S(1)}, u32[]{:S(2)}, u32[]{:S(2)}) %collective-permute-start.6) | collective-permute-done | bytes 393248 | tf_op jit(solution)/shard_map/ppermute | solution.py:137
  79.6 0.7 copy-done.4
  80.7 1.9 collective-permute-start.3
  82.7 15.8 %collective-permute-done.3 = f32[8,16512]{1,0:T(8,128)S(1)} collective-permute-done((f32[8,16512]{1,0:T(8,128)S(1)}, f32[8,16512]{1,0:T(8,128)S(1)}, u32[]{:S(2)}, u32[]{:S(2)}) %collective-permute-start.3) | collective-permute-done | bytes 528416 | tf_op jit(solution)/shard_map/ppermute | solution.py:94
  98.7 1.9 collective-permute-start.4
  100.8 20.9 %collective-permute-done.4 = f32[8,16512]{1,0:T(8,128)S(1)} collective-permute-done((f32[8,16512]{1,0:T(8,128)S(1)}, f32[8,16512]{1,0:T(8,128)S(1)}, u32[]{:S(2)}, u32[]{:S(2)}) %collective-permute-start.4) | collective-permute-done | bytes 528416 | tf_op jit(solution)/shard_map/ppermute | solution.py:94
  121.9 1.3 collective-permute-start.5
  123.4 0.7 fusion.2
  124.1 10.8 %collective-permute-done.5 = f32[8,16512]{1,0:T(8,128)S(1)} collective-permute-done((f32[8,16512]{1,0:T(8,128)S(1)}, f32[8,16512]{1,0:T(8,128)S(1)}, u32[]{:S(2)}, u32[]{:S(2)}) %collective-permute-start.5) | collective-permute-done | bytes 528416 | tf_op jit(solution)/shard_map/ppermute | solution.py:94
  135.2 0.6 fusion.3
  136.0 0.5 multiply_reduce_fusion
  136.9 0.7 copy-done.5
  137.8 7.7 %collective-permute-done.7 = bf16[128,1024]{1,0:T(8,128)(2,1)S(1)} collective-permute-done((bf16[128,1024]{1,0:T(8,128)(2,1)S(1)}, bf16[128,1024]{1,0:T(8,128)(2,1)S(1)}, u32[]{:S(2)}, u32[]{:S(2)}) %collective-permute-start.7) | collective-permute-done | bytes 262176 | tf_op jit(solution)/shard_map/ppermute | solution.py:16
  145.5 16.1 %collective-permute-start.8 = (bf16[128,1024]{1,0:T(8,128)(2,1)S(1)}, bf16[128,1024]{1,0:T(8,128)(2,1)S(1)}, u32[]{:S(2)}, u32[]{:S(2)}) collective-permute-start(bf16[128,1024]{1,0:T(8,128)(2,1)S(1)} %collective-permute-done.7), channel_id=1, source_target_pairs={{0,7},{1,0},{2,1},{3,2},{4,3},{5,4},{6,5},{7,6},{8,15},{9,8},{10,9... | collective-permute-start | bytes 786440 | tf_op jit(solution)/shard_map/ppermute | solution.py:16
  161.6 6.3 %collective-permute-done.8 = bf16[128,1024]{1,0:T(8,128)(2,1)S(1)} collective-permute-done((bf16[128,1024]{1,0:T(8,128)(2,1)S(1)}, bf16[128,1024]{1,0:T(8,128)(2,1)S(1)}, u32[]{:S(2)}, u32[]{:S(2)}) %collective-permute-start.8) | collective-permute-done | bytes 262176 | tf_op jit(solution)/shard_map/ppermute | solution.py:16
  167.8 3.7 %collective-permute-start.9 = (bf16[128,1024]{1,0:T(8,128)(2,1)S(1)}, bf16[128,1024]{1,0:T(8,128)(2,1)S(1)}, u32[]{:S(2)}, u32[]{:S(2)}) collective-permute-start(bf16[128,1024]{1,0:T(8,128)(2,1)S(1)} %collective-permute-done.8), channel_id=1, source_target_pairs={{0,7},{1,0},{2,1},{3,2},{4,3},{5,4},{6,5},{7,6},{8,15},{9,8},{10,9... | collective-permute-start | bytes 786440 | tf_op jit(solution)/shard_map/ppermute | solution.py:16
  171.5 5.4 %collective-permute-done.9 = bf16[128,1024]{1,0:T(8,128)(2,1)S(1)} collective-permute-done((bf16[128,1024]{1,0:T(8,128)(2,1)S(1)}, bf16[128,1024]{1,0:T(8,128)(2,1)S(1)}, u32[]{:S(2)}, u32[]{:S(2)}) %collective-permute-start.9) | collective-permute-done | bytes 262176 | tf_op jit(solution)/shard_map/ppermute | solution.py:16
  176.9 3.7 %collective-permute-start.10 = (bf16[128,1024]{1,0:T(8,128)(2,1)S(1)}, bf16[128,1024]{1,0:T(8,128)(2,1)S(1)}, u32[]{:S(2)}, u32[]{:S(2)}) collective-permute-start(bf16[128,1024]{1,0:T(8,128)(2,1)S(1)} %collective-permute-done.9), channel_id=1, source_target_pairs={{0,7},{1,0},{2,1},{3,2},{4,3},{5,4},{6,5},{7,6},{8,15},{9,8},{10,9... | collective-permute-start | bytes 786440 | tf_op jit(solution)/shard_map/ppermute | solution.py:16
  180.6 4.5 %collective-permute-done.10 = bf16[128,1024]{1,0:T(8,128)(2,1)S(1)} collective-permute-done((bf16[128,1024]{1,0:T(8,128)(2,1)S(1)}, bf16[128,1024]{1,0:T(8,128)(2,1)S(1)}, u32[]{:S(2)}, u32[]{:S(2)}) %collective-permute-start.10) | collective-permute-done | bytes 262176 | tf_op jit(solution)/shard_map/ppermute | solution.py:16
  185.2 3.7 %collective-permute-start.11 = (bf16[128,1024]{1,0:T(8,128)(2,1)S(1)}, bf16[128,1024]{1,0:T(8,128)(2,1)S(1)}, u32[]{:S(2)}, u32[]{:S(2)}) collective-permute-start(bf16[128,1024]{1,0:T(8,128)(2,1)S(1)} %collective-permute-done.10), channel_id=1, source_target_pairs={{0,7},{1,0},{2,1},{3,2},{4,3},{5,4},{6,5},{7,6},{8,15},{9,8},{10,9... | collective-permute-start | bytes 786440 | tf_op jit(solution)/shard_map/ppermute | solution.py:16
  188.9 3.9 %collective-permute-done.11 = bf16[128,1024]{1,0:T(8,128)(2,1)S(1)} collective-permute-done((bf16[128,1024]{1,0:T(8,128)(2,1)S(1)}, bf16[128,1024]{1,0:T(8,128)(2,1)S(1)}, u32[]{:S(2)}, u32[]{:S(2)}) %collective-permute-start.11) | collective-permute-done | bytes 262176 | tf_op jit(solution)/shard_map/ppermute | solution.py:16
  192.7 3.7 %collective-permute-start.12 = (bf16[128,1024]{1,0:T(8,128)(2,1)S(1)}, bf16[128,1024]{1,0:T(8,128)(2,1)S(1)}, u32[]{:S(2)}, u32[]{:S(2)}) collective-permute-start(bf16[128,1024]{1,0:T(8,128)(2,1)S(1)} %collective-permute-done.11), channel_id=1, source_target_pairs={{0,7},{1,0},{2,1},{3,2},{4,3},{5,4},{6,5},{7,6},{8,15},{9,8},{10,9... | collective-permute-start | bytes 786440 | tf_op jit(solution)/shard_map/ppermute | solution.py:16
  196.4 3.9 %collective-permute-done.12 = bf16[128,1024]{1,0:T(8,128)(2,1)S(1)} collective-permute-done((bf16[128,1024]{1,0:T(8,128)(2,1)S(1)}, bf16[128,1024]{1,0:T(8,128)(2,1)S(1)}, u32[]{:S(2)}, u32[]{:S(2)}) %collective-permute-start.12) | collective-permute-done | bytes 262176 | tf_op jit(solution)/shard_map/ppermute | solution.py:16
  200.3 3.7 %collective-permute-start.13 = (bf16[128,1024]{1,0:T(8,128)(2,1)S(1)}, bf16[128,1024]{1,0:T(8,128)(2,1)S(1)}, u32[]{:S(2)}, u32[]{:S(2)}) collective-permute-start(bf16[128,1024]{1,0:T(8,128)(2,1)S(1)} %collective-permute-done.12), channel_id=1, source_target_pairs={{0,7},{1,0},{2,1},{3,2},{4,3},{5,4},{6,5},{7,6},{8,15},{9,8},{10,9... | collective-permute-start | bytes 786440 | tf_op jit(solution)/shard_map/ppermute | solution.py:16
  204.0 21.3 %reshape.83 = bf16[4,8192,192]{1,0,2:T(4,128)(2,1)} reshape(bf16[32768,192]{0,1:T(8,128)(2,1)} %all-gather.2.cloned.1.call-done) | data formatting | bytes 25165824 | tf_op jit(solution)/shard_map/reshape | solution.py:139
  225.3 7.5 %constant_dynamic-slice_fusion.6 = (bf16[4,1024,192]{1,0,2:T(4,128)(2,1)S(1)}, bf16[4,1024,192]{1,0,2:T(4,128)(2,1)S(1)}, bf16[4,1024,192]{1,0,2:T(4,128)(2,1)S(...) fusion(bf16[4,8192,192]{1,0,2:T(4,128)(2,1)} %reshape.83, ...), kind=kLoop, calls=%fused_computation.79 | loop fusion | bytes 25165856 | tf_op jit(solution)/shard_map/dynamic_slice | solution.py:146
  232.8 0.5 copy.78
  233.3 0.5 copy.77
  233.8 0.5 copy.76
  234.2 0.5 copy.75
  236.6 0.6 fusion.41
  237.2 0.6 fusion.47
  237.8 0.6 fusion.46
  238.3 0.6 fusion.45
  238.9 0.6 fusion.44
  239.5 0.6 fusion.43
  240.1 0.6 fusion.42
  240.7 0.6 fusion.48
  241.4 0.9 copy.69
  (62 shorter events, 5.5 us)
Async XLA Ops:
  6.5 116.8 %copy-start = (bf16[128,1024]{1,0:T(8,128)(2,1)S(1)}, bf16[128,1024]{1,0:T(8,128)(2,1)}, u32[]{:S(2)}) copy-start(bf16[128,1024]{1,0:T(8,128)(2,1)} %param.8) | copy-start | bytes 786436
  6.5 197.5 %all-gather.2.cloned.1.call-start = ((), (), s32[]{:S(2)}) async-start(), calls=%async_computation | async-start | bytes 12976128 | tf_op jit(solution)/shard_map/all_gather | solution.py:138
  8.8 3.8 %copy-start.3 = (f32[8,128,128]{2,1,0:T(8,128)S(1)}, f32[8,128,128]{2,1,0:T(8,128)}, u32[]{:S(2)}) copy-start(f32[8,128,128]{2,1,0:T(8,128)} %param.13) | copy-start | bytes 1572868
  10.6 12.7 %collective-permute-start = (f32[8,16512]{1,0:T(8,128)S(1)}, f32[8,16512]{1,0:T(8,128)S(1)}, u32[]{:S(2)}, u32[]{:S(2)}) collective-permute-start(f32[8,16512]{1,0:T(8,128)S(1)} %pad_maximum_fusion), channel_id=1, source_target_pairs={{0,8},{8,16},{16,24},{24,32},{32,40},{40,48},{48,56},{56,64},{64,7... | collective-permute-start | bytes 1585160 | tf_op jit(solution)/shard_map/ppermute | solution.py:89
  23.4 12.7 %collective-permute-start.1 = (f32[8,16512]{1,0:T(8,128)S(1)}, f32[8,16512]{1,0:T(8,128)S(1)}, u32[]{:S(2)}, u32[]{:S(2)}) collective-permute-start(f32[8,16512]{1,0:T(8,128)S(1)} %pad_select_fusion), channel_id=1, source_target_pairs={{0,8},{8,16},{16,24},{24,32},{32,40},{40,48},{48,56},{56,64},{64,7... | collective-permute-start | bytes 1585160 | tf_op jit(solution)/shard_map/ppermute | solution.py:94
  36.0 2.1 copy-start.7
  36.2 44.2 %collective-permute-start.2 = (f32[8,16512]{1,0:T(8,128)S(1)}, f32[8,16512]{1,0:T(8,128)S(1)}, u32[]{:S(2)}, u32[]{:S(2)}) collective-permute-start(f32[8,16512]{1,0:T(8,128)S(1)} %maximum_select_fusion), channel_id=1, source_target_pairs={{0,16},{8,24},{16,32},{24,40},{32,48},{40,56},{48,64},{56,72},{64,... | collective-permute-start | bytes 1585160 | tf_op jit(solution)/shard_map/ppermute | solution.py:94
  38.2 41.4 %collective-permute-start.6 = (bf16[1024,192]{0,1:T(8,128)(2,1)S(1)}, bf16[1024,192]{0,1:T(8,128)(2,1)S(1)}, u32[]{:S(2)}, u32[]{:S(2)}) collective-permute-start(bf16[1024,192]{0,1:T(8,128)(2,1)S(1)} %copy-done.7), channel_id=1, source_target_pairs={{0,0},{32,1},{64,2},{96,3},{128,4},{160,5},{192,6},{224,7},{1,8},{... | collective-permute-start | bytes 1179656 | tf_op jit(solution)/shard_map/ppermute | solution.py:137
  79.6 0.7 copy-start.4
  80.7 17.9 %collective-permute-start.3 = (f32[8,16512]{1,0:T(8,128)S(1)}, f32[8,16512]{1,0:T(8,128)S(1)}, u32[]{:S(2)}, u32[]{:S(2)}) collective-permute-start(f32[8,16512]{1,0:T(8,128)S(1)} %maximum_select_fusion.1), channel_id=1, source_target_pairs={{0,32},{8,40},{16,48},{24,56},{32,64},{40,72},{48,80},{56,88},{64,... | collective-permute-start | bytes 1585160 | tf_op jit(solution)/shard_map/ppermute | solution.py:94
  98.7 22.9 %collective-permute-start.4 = (f32[8,16512]{1,0:T(8,128)S(1)}, f32[8,16512]{1,0:T(8,128)S(1)}, u32[]{:S(2)}, u32[]{:S(2)}) collective-permute-start(f32[8,16512]{1,0:T(8,128)S(1)} %maximum_select_fusion.2), channel_id=1, source_target_pairs={{0,64},{8,72},{16,80},{24,88},{32,96},{40,104},{48,112},{56,120},{... | collective-permute-start | bytes 1585160 | tf_op jit(solution)/shard_map/ppermute | solution.py:94
  121.9 13.1 %collective-permute-start.5 = (f32[8,16512]{1,0:T(8,128)S(1)}, f32[8,16512]{1,0:T(8,128)S(1)}, u32[]{:S(2)}, u32[]{:S(2)}) collective-permute-start(f32[8,16512]{1,0:T(8,128)S(1)} %maximum_select_fusion.3), channel_id=1, source_target_pairs={{0,128},{8,136},{16,144},{24,152},{32,160},{40,168},{48,176},{56,1... | collective-permute-start | bytes 1585160 | tf_op jit(solution)/shard_map/ppermute | solution.py:94
  135.1 1.0 copy-start.2
  136.6 1.0 copy-start.5
  136.6 0.9 copy-start.6
  137.7 7.8 %collective-permute-start.7 = (bf16[128,1024]{1,0:T(8,128)(2,1)S(1)}, bf16[128,1024]{1,0:T(8,128)(2,1)S(1)}, u32[]{:S(2)}, u32[]{:S(2)}) collective-permute-start(bf16[128,1024]{1,0:T(8,128)(2,1)S(1)} %multiply_convert_fusion), channel_id=1, source_target_pairs={{0,7},{1,0},{2,1},{3,2},{4,3},{5,4},{6,5},{7,6},{8,15},{9,8},{10,9... | collective-permute-start | bytes 786440 | tf_op jit(solution)/shard_map/ppermute | solution.py:16
  145.5 22.3 %collective-permute-start.8 = (bf16[128,1024]{1,0:T(8,128)(2,1)S(1)}, bf16[128,1024]{1,0:T(8,128)(2,1)S(1)}, u32[]{:S(2)}, u32[]{:S(2)}) collective-permute-start(bf16[128,1024]{1,0:T(8,128)(2,1)S(1)} %collective-permute-done.7), channel_id=1, source_target_pairs={{0,7},{1,0},{2,1},{3,2},{4,3},{5,4},{6,5},{7,6},{8,15},{9,8},{10,9... | collective-permute-start | bytes 786440 | tf_op jit(solution)/shard_map/ppermute | solution.py:16
  167.8 9.1 %collective-permute-start.9 = (bf16[128,1024]{1,0:T(8,128)(2,1)S(1)}, bf16[128,1024]{1,0:T(8,128)(2,1)S(1)}, u32[]{:S(2)}, u32[]{:S(2)}) collective-permute-start(bf16[128,1024]{1,0:T(8,128)(2,1)S(1)} %collective-permute-done.8), channel_id=1, source_target_pairs={{0,7},{1,0},{2,1},{3,2},{4,3},{5,4},{6,5},{7,6},{8,15},{9,8},{10,9... | collective-permute-start | bytes 786440 | tf_op jit(solution)/shard_map/ppermute | solution.py:16
  176.9 8.2 %collective-permute-start.10 = (bf16[128,1024]{1,0:T(8,128)(2,1)S(1)}, bf16[128,1024]{1,0:T(8,128)(2,1)S(1)}, u32[]{:S(2)}, u32[]{:S(2)}) collective-permute-start(bf16[128,1024]{1,0:T(8,128)(2,1)S(1)} %collective-permute-done.9), channel_id=1, source_target_pairs={{0,7},{1,0},{2,1},{3,2},{4,3},{5,4},{6,5},{7,6},{8,15},{9,8},{10,9... | collective-permute-start | bytes 786440 | tf_op jit(solution)/shard_map/ppermute | solution.py:16
  185.2 7.6 %collective-permute-start.11 = (bf16[128,1024]{1,0:T(8,128)(2,1)S(1)}, bf16[128,1024]{1,0:T(8,128)(2,1)S(1)}, u32[]{:S(2)}, u32[]{:S(2)}) collective-permute-start(bf16[128,1024]{1,0:T(8,128)(2,1)S(1)} %collective-permute-done.10), channel_id=1, source_target_pairs={{0,7},{1,0},{2,1},{3,2},{4,3},{5,4},{6,5},{7,6},{8,15},{9,8},{10,9... | collective-permute-start | bytes 786440 | tf_op jit(solution)/shard_map/ppermute | solution.py:16
  192.7 7.6 %collective-permute-start.12 = (bf16[128,1024]{1,0:T(8,128)(2,1)S(1)}, bf16[128,1024]{1,0:T(8,128)(2,1)S(1)}, u32[]{:S(2)}, u32[]{:S(2)}) collective-permute-start(bf16[128,1024]{1,0:T(8,128)(2,1)S(1)} %collective-permute-done.11), channel_id=1, source_target_pairs={{0,7},{1,0},{2,1},{3,2},{4,3},{5,4},{6,5},{7,6},{8,15},{9,8},{10,9... | collective-permute-start | bytes 786440 | tf_op jit(solution)/shard_map/ppermute | solution.py:16
  200.3 40.4 %collective-permute-start.13 = (bf16[128,1024]{1,0:T(8,128)(2,1)S(1)}, bf16[128,1024]{1,0:T(8,128)(2,1)S(1)}, u32[]{:S(2)}, u32[]{:S(2)}) collective-permute-start(bf16[128,1024]{1,0:T(8,128)(2,1)S(1)} %collective-permute-done.12), channel_id=1, source_target_pairs={{0,7},{1,0},{2,1},{3,2},{4,3},{5,4},{6,5},{7,6},{8,15},{9,8},{10,9... | collective-permute-start | bytes 786440 | tf_op jit(solution)/shard_map/ppermute | solution.py:16
  241.3 1.1 copy-start.1
Sparse Core Ops, SparseCore 0:
  80.5 88.5 all-gather.1
